TPU v7x, 32 devices: a whole 2x2x4 slice. The times are simulated.
32 devices in a mesh: dp: 8 (over z, y), group: 4 (over x, core).
Axes of the slice: x: 2, y: 2, z: 4, core: 2. Of those that a mesh axis runs over, the one named last changes fastest.
Arguments:
- gradients: float32 [32, 3, 320, 960], P(('dp', 'group')), may hold values from -0.8 to 0.8
- errors: bfloat16 [32, 3, 320, 960], P(('dp', 'group')), may hold values from -0.59765625 to 0.59765625
- q_init: float32 [3, 960, 32], replicated, may hold values from -0.1875 to 0.1875
- owners: int32 [3], replicated, may hold values from 0 to 31, as said below
- buckets: int32 [3], replicated, may hold values from 0 to 3
- learn_rates: float32 [4], replicated, may hold values from 0.2 to 1
- beta_values: float32 [4], replicated, may hold values from 0.5 to 0.95
- momentum: bfloat16 [64, 320, 960], P(('dp', 'group')), may hold values from -3 to 3
Outputs:
- new_errors: bfloat16 [32, 3, 320, 960], P(('dp', 'group'))
- weight_steps: bfloat16 [32, 3, 320, 960], P(('dp', 'group'))
- new_momentum: bfloat16 [64, 320, 960], P(('dp', 'group'))
Inputs may be any that keep to these rules, and one draw needn't show every extreme that they name: `owners`: no device owns more than 2 matrices, and some device owns exactly 2.
All inputs are finite; a program needn't handle non-finite values.
Results may differ from a plain program's by a relative error of at most 0.001.
Values may be sent and summed in bfloat16 or wider, within the bound.
No kernel may reach another device: no remote copies, remote signals or barrier semaphores. Data moves between devices by JAX's collectives and lax.ppermute only.
A program may use at most 64 MiB of HBM per device.

v0:
```python
import jax
import jax.numpy as jnp
from jax import lax
from jax.sharding import PartitionSpec as P


def from_root(value, axis, source):
    kept = jnp.where(lax.axis_index(axis) == source, value, 0).astype(value.dtype)
    return lax.psum(kept, axis)


def on_device(gradients, errors, q_init, owners, buckets, learn_rates, beta_values, momentum):
    highest = lax.Precision.HIGHEST
    slot_count = momentum.shape[0]
    mat_count = owners.shape[0]
    bucket_count = learn_rates.shape[0]
    my_index = lax.axis_index(("dp", "group"))
    positions = jnp.arange(mat_count, dtype=jnp.int32)
    earlier = (owners[None, :] == owners[:, None]) & (positions[None, :] < positions[:, None])
    slot_list = jnp.sum(earlier.astype(jnp.int32), axis=1)
    bucket_hits = buckets[:, None] == jnp.arange(bucket_count, dtype=jnp.int32)[None, :]
    rate_list = jnp.sum(jnp.where(bucket_hits, learn_rates[None, :], 0.0), axis=1)
    beta_list = jnp.sum(jnp.where(bucket_hits, beta_values[None, :], 0.0), axis=1)
    merged = gradients[0] + errors[0].astype(jnp.float32)
    p_local = jnp.einsum("mkd,mdr->mkr", merged, q_init, precision=highest)
    p_sum = lax.psum(p_local, ("dp", "group"))
    gram_matrix = jnp.einsum("mkr,mks->mrs", p_sum, p_sum, precision=highest)
    lower_factor = jnp.linalg.cholesky(gram_matrix)
    p_hat = lax.linalg.triangular_solve(
        lower_factor, p_sum, left_side=False, lower=True, transpose_a=True
    )
    q_local = jnp.einsum("mkd,mkr->mdr", merged, p_hat, precision=highest)
    q_sum = lax.psum(q_local, ("dp", "group"))
    approx = jnp.einsum("mkr,mdr->mkd", p_hat, q_local, precision=highest)
    new_errors = (merged - approx).astype(jnp.bfloat16)
    update = jnp.einsum("mkr,mdr->mkd", p_hat, q_sum, precision=highest)
    slot_range = jnp.arange(slot_count, dtype=jnp.int32)
    new_slab = jnp.zeros(momentum.shape, jnp.float32)
    step_list = []
    for matrix in range(mat_count):
        old_state = lax.dynamic_index_in_dim(momentum, slot_list[matrix], 0, keepdims=False).astype(
            jnp.float32
        )
        mom_new = beta_list[matrix] * old_state + update[matrix]
        step_value = (-rate_list[matrix] * (update[matrix] + beta_list[matrix] * mom_new)).astype(
            jnp.bfloat16
        )
        step_value = from_root(step_value, ("dp", "group"), owners[matrix])
        step_list.append(step_value)
        selected = (slot_range == slot_list[matrix]) & (owners[matrix] == my_index)
        new_slab = new_slab + jnp.where(selected[:, None, None], mom_new[None], 0.0)
    return (new_errors[None], jnp.stack(step_list)[None], new_slab.astype(jnp.bfloat16))


def solution(mesh):
    placed = (
        P(("dp", "group"), None, None, None),
        P(("dp", "group"), None, None, None),
        P(),
        P(),
        P(),
        P(),
        P(),
        P(("dp", "group"), None, None),
    )
    return jax.shard_map(
        on_device,
        mesh=mesh,
        in_specs=placed,
        out_specs=(
            P(("dp", "group"), None, None, None),
            P(("dp", "group"), None, None, None),
            P(("dp", "group"), None, None),
        ),
        check_vma=False,
    )
```

profile of v0, /device:TPU:0, one launch (start us, length us, event | category | flops | bytes accessed | tf_op | source)
XLA Modules:
  0.0 456.5 jit_solution(16836187007871859211)
XLA Ops:
  7.2 0.0 copy-start
  7.2 0.0 copy-start.5
  7.2 0.0 all-reduce.5.cloned.1.call-start
  7.2 0.9 copy-done
  8.2 7.3 %fusion.2 = f32[3,320,32]{1,2,0:T(8,128)} fusion(f32[3,960,32]{1,2,0:T(8,128)S(1)} %copy-done, f32[1,3,320,960]{3,2,1,0:T(8,128)} %param.8, bf16[1,3,320,960]{3,2,1,0:T(8,128)(2,1)} %param.9), kind=kOutput, calls=%fused_computation.3 | convolution fusion | flops 355737600 | bytes 6021120 | tf_op jit(solution)/shard_map/mkd,mdr->mkr/dot_general | solution.py:25
  15.5 0.0 all-reduce.5.cloned.1.call-update
  15.5 0.0 copy-done.5
  15.5 0.2 convert_reduce_fusion
  15.7 0.7 fusion.28
  20.2 0.6 fusion.29
  24.7 114.3 %all-reduce.5.cloned.1.call-done = f32[3,320,32]{1,2,0:T(8,128)} async-done(((f32[3,320,32]{1,2,0:T(8,128)}), f32[3,320,32]{1,2,0:T(8,128)}) %all-reduce.5.cloned.1.call-update) | async-done | bytes 122896 | tf_op jit(solution)/shard_map/psum | solution.py:26
  139.0 1.3 fusion.32
  140.3 0.1 copy.13
  140.4 8.8 %custom-call.7 = f32[3,32,32]{2,1,0:T(8,128)S(1)} custom-call(f32[3,32,32]{2,1,0:T(8,128)S(1)} %fusion.26), custom_call_target="Cholesky" | custom-call | tf_op jit(solution)/shard_map/jit(cholesky)/cholesky | solution.py:28
  149.2 0.1 compare_reduce_fusion
  149.3 0.1 select_bitcast_fusion
  149.4 7.4 %custom-call.8 = f32[3,1,32,32]{2,3,1,0:T(8,128)S(1)} custom-call(f32[3,1,32,32]{3,2,1,0:T(8,128)S(1)} %select_bitcast_fusion), custom_call_target="InvertDiagBlocksLowerTriangular" | custom-call | tf_op jit(solution)/shard_map/triangular_solve | solution.py:29
  156.8 1.3 fusion.24
  158.0 0.0 copy-done.2
  158.1 4.8 %fusion = f32[3,960,32]{1,2,0:T(8,128)S(1)} fusion(f32[3,320,32]{1,2,0:T(8,128)S(1)} %fusion.24, f32[1,3,320,960]{3,2,1,0:T(8,128)} %param.8, bf16[1,3,320,960]{3,2,1,0:T(8,128)(2,1)S(1)} %copy-done.2), kind=kOutput, calls=%fused_computation.1 | convolution fusion | flops 355737600 | bytes 6021120 | tf_op jit(solution)/shard_map/mkd,mkr->mdr/dot_general | solution.py:32
  162.9 0.0 copy-start.4
  162.9 0.0 copy-start.6
  162.9 0.0 copy-start.7
  162.9 0.0 copy-start.8
  162.9 6.3 %fusion.5 = bf16[1,3,320,960]{3,2,1,0:T(8,128)(2,1)} fusion(f32[3,320,32]{1,2,0:T(8,128)S(1)} %fusion.24, f32[3,960,32]{1,2,0:T(8,128)S(1)} %fusion, f32[1,3,320,960]{3,2,1,0:T(8,128)} %param.8, bf16[1,3,320,960]{3,2,1,0:T(8,128)(2,1)S(1)} %copy-done.2), kind=kOutput, calls=%fused_computation.9 | convolution fusion | flops 357580800 | bytes 7864320 | tf_op jit(solution)/shard_map/mkr,mdr->mkd/dot_general | solution.py:34
  169.2 0.0 copy-done.4
  169.2 0.0 all-reduce.7.cloned.1.call-start
  169.3 0.7 all-reduce.7.cloned.1.call-update
  170.0 0.2 all-reduce.9.cloned.1.call-start
  170.2 0.0 copy-done.6
  170.2 0.0 copy-done.7
  170.2 0.0 copy-done.8
  170.2 0.2 select_reduce_fusion.2
  170.4 0.7 fusion.30
  174.9 0.0 copy-start.3
  174.9 130.5 %all-reduce.7.cloned.1.call-done = f32[3,960,32]{1,2,0:T(8,128)} async-done(((f32[3,960,32]{1,2,0:T(8,128)}), f32[3,960,32]{1,2,0:T(8,128)}) %all-reduce.7.cloned.1.call-update) | async-done | bytes 368656 | tf_op jit(solution)/shard_map/psum | solution.py:33
  305.4 4.3 fusion.33
  309.7 0.0 copy-start.1
  309.7 0.0 copy-done.3
  309.7 3.9 fusion.19
  313.6 0.0 copy-done.1
  313.6 0.0 all-reduce.9.cloned.1.call-update
  313.6 0.6 compare_and_fusion.2
  314.2 1.3 compare_and_fusion
  315.5 4.8 %add_bitcast_fusion.2 = (f32[320,960]{1,0:T(8,128)S(1)}, f32[320,960]{1,0:T(8,128)S(1)}, f32[320,960]{1,0:T(8,128)S(1)}) fusion(f32[3,320,960]{2,1,0:T(8,128)} %copy-done.1, f32[]{:T(128)} %bitcast.8, bf16[2,320,960]{2,1,0:T(8,128)(2,1)S(1)} %copy-done.3, s32[]{:T(128)S(6)} %select_n.55, s32[]{:T(128)S(6)} %select_n.58, f32[]{:T(128)} %bitcast.15, ...), kind=kLoop, calls=%fused_computation.27 | loop fusion | flops 2764800 | bytes 9216024 | tf_op jit(solution)/shard_map/jit(_where)/broadcast_in_dim | solution.py:51
  320.4 1.7 add_convert_fusion
  322.1 125.0 %all-reduce.9.cloned.1.call-done = (bf16[1,320,960]{2,1,0:T(8,128)(2,1)}, bf16[1,320,960]{2,1,0:T(8,128)(2,1)}, bf16[1,320,960]{2,1,0:T(8,128)(2,1)}) async-done(((bf16[1,320,960]{2,1,0:T(8,128)(2,1)}, bf16[1,320,960]{2,1,0:T(8,128)(2,1)}, bf16[1,320,960]{2,1,0:T(8,128)(2,1)}), (bf16[1,320,960]{2,1,0:T(8,128)(2,1)}, bf16[1,320,960]{2,1,0:T(8,128)(2,1)}, ...) | async-done | bytes 1843216 | tf_op jit(solution)/shard_map/psum | solution.py:9
  447.0 3.0 maximum_bitcast_fusion
  (5 shorter events, 0.1 us)
Async XLA Ops:
  7.2 1.0 copy-start
  7.2 8.3 %copy-start.5 = (s32[3]{0:T(128)S(1)}, s32[3]{0:T(128)}, u32[]{:S(2)}) copy-start(s32[3]{0:T(128)} %param.11) | copy-start | bytes 40
  7.2 131.8 %all-reduce.5.cloned.1.call-start = ((), (), s32[]{:S(2)}) async-start(), calls=%async_computation | async-start | bytes 294912 | tf_op jit(solution)/shard_map/psum | solution.py:26
  8.2 149.9 %copy-start.2 = (bf16[1,3,320,960]{3,2,1,0:T(8,128)(2,1)S(1)}, bf16[1,3,320,960]{3,2,1,0:T(8,128)(2,1)}, u32[]{:S(2)}) copy-start(bf16[1,3,320,960]{3,2,1,0:T(8,128)(2,1)} %param.9) | copy-start | bytes 5529604
  162.9 6.4 %copy-start.4 = (f32[3,960,32]{1,2,0:T(8,128)}, f32[3,960,32]{1,2,0:T(8,128)S(1)}, u32[]{:S(2)}) copy-start(f32[3,960,32]{1,2,0:T(8,128)S(1)} %fusion) | copy-start | bytes 1105924
  162.9 7.3 %copy-start.6 = (f32[4]{0:T(128)S(1)}, f32[4]{0:T(128)}, u32[]{:S(2)}) copy-start(f32[4]{0:T(128)} %param.13) | copy-start | bytes 52
  162.9 7.3 %copy-start.7 = (s32[3]{0:T(128)S(1)}, s32[3]{0:T(128)}, u32[]{:S(2)}) copy-start(s32[3]{0:T(128)} %param.12) | copy-start | bytes 40
  162.9 7.3 %copy-start.8 = (f32[4]{0:T(128)S(1)}, f32[4]{0:T(128)}, u32[]{:S(2)}) copy-start(f32[4]{0:T(128)} %param.14) | copy-start | bytes 52
  169.2 136.1 %all-reduce.7.cloned.1.call-start = ((), (), s32[]{:S(2)}) async-start(), calls=%async_computation.1 | async-start | bytes 786432 | tf_op jit(solution)/shard_map/psum | solution.py:33
  170.0 277.0 %all-reduce.9.cloned.1.call-start = ((), (), s32[]{:S(2)}) async-start(), calls=%async_computation.2 | async-start | bytes 3932160 | tf_op jit(solution)/shard_map/psum | solution.py:9
  174.9 134.8 %copy-start.3 = (bf16[2,320,960]{2,1,0:T(8,128)(2,1)S(1)}, bf16[2,320,960]{2,1,0:T(8,128)(2,1)}, u32[]{:S(2)}) copy-start(bf16[2,320,960]{2,1,0:T(8,128)(2,1)} %param.15) | copy-start | bytes 3686404
  309.7 3.9 copy-start.1
Sparse Core Ops, SparseCore 0:
  15.6 123.3 all-reduce.4
  175.9 129.3 all-reduce.6
  313.7 133.2 all-reduce.8
where the time goes:
time: 457 us
  waiting for transfers between devices  371 us (81%)
  other arithmetic  32.1 us (7%)
  between operations  25.4 us (6%)
  matrix products  25.2 us (6%)
    psum x1, waiting for transfers between devices, on_device(): q_sum = lax.psum(q_local, ('dp', 'group'))  131 us
    psum x1, waiting for transfers between devices, from_root(): return lax.psum(kept, axis)  125 us
    psum x1, waiting for transfers between devices, on_device(): p_sum = lax.psum(p_local, ('dp', 'group'))  114 us
  transfers between devices with their start and end apart: 3, of which 3 were waited for; matrix products, arithmetic and copies ran while one was open for 2% of the time, Pallas kernels for 0%

commit v1 on v0

--- a/solution.py
+++ b/solution.py
@@ -23,7 +23,7 @@
     beta_list = jnp.sum(jnp.where(bucket_hits, beta_values[None, :], 0.0), axis=1)
     merged = gradients[0] + errors[0].astype(jnp.float32)
     p_local = jnp.einsum("mkd,mdr->mkr", merged, q_init, precision=highest)
-    p_sum = lax.psum(p_local, ("dp", "group"))
+    p_sum = jnp.sum(lax.all_gather(p_local, ("dp", "group")), axis=0)
     gram_matrix = jnp.einsum("mkr,mks->mrs", p_sum, p_sum, precision=highest)
     lower_factor = jnp.linalg.cholesky(gram_matrix)
     p_hat = lax.linalg.triangular_solve(

time: 457 us -> 398 us (0.87)
  waiting for transfers between devices: 371 us -> 310 us
    psum x1 -> x0, waiting for transfers between devices: 114 us -> none  [on_device(): p_sum = lax.psum(p_local, ('dp', 'group'))]
    all_gather x0 -> x1, waiting for transfers between devices: none -> 57.3 us  [on_device(): p_sum = jnp.sum(lax.all_gather(p_local, ('dp', 'group')), axis=0)]
  transfers between devices with their start and end apart: 3 -> 3, of which waited for: 3 -> 3; matrix products, arithmetic and copies ran while one was open for 2% -> 3% of each run, Pallas kernels for 0% -> 0%
where the time goes in v1:
time: 398 us; the launch traced here: 397 us
  waiting for transfers between devices  310 us (78%)
  other arithmetic  34.9 us (9%)
  between operations  25.4 us (6%)
  matrix products  23.2 us (6%)
    psum x1, waiting for transfers between devices, on_device(): q_sum = lax.psum(q_local, ('dp', 'group'))  127 us
    psum x1, waiting for transfers between devices, from_root(): return lax.psum(kept, axis)  125 us
    all_gather x1, waiting for transfers between devices, on_device(): p_sum = jnp.sum(lax.all_gather(p_local, ('dp', 'group')), axis=0)  57.3 us
    another operation x4, other arithmetic, on_device(): lower_factor = jnp.linalg.cholesky(gram_matrix)  8.96 us
  transfers between devices with their start and end apart: 3, of which 3 were waited for; matrix products, arithmetic and copies ran while one was open for 3% of the time, Pallas kernels for 0%

profile of v1, /device:TPU:0, one launch (start us, length us, event | category | flops | bytes accessed | tf_op | source)
XLA Modules:
  0.0 397.1 jit_solution(1436154054713227769)
XLA Ops:
  7.2 0.0 copy-start
  7.2 0.0 copy-start.5
  7.2 0.0 all-gather.3.cloned.1.call-start
  7.2 0.9 copy-done
  8.2 7.2 %fusion.2 = f32[3,320,32]{1,2,0:T(8,128)} fusion(f32[3,960,32]{1,2,0:T(8,128)S(1)} %copy-done, f32[1,3,320,960]{3,2,1,0:T(8,128)} %param.8, bf16[1,3,320,960]{3,2,1,0:T(8,128)(2,1)} %param.9), kind=kOutput, calls=%fused_computation.3 | convolution fusion | flops 355737600 | bytes 6021120 | tf_op jit(solution)/shard_map/mkd,mdr->mkr/dot_general | solution.py:25
  15.3 0.0 all-gather.3.cloned.1.call-update
  15.3 0.0 copy-done.5
  15.4 0.2 convert_reduce_fusion
  15.5 0.7 fusion.28
  20.0 0.6 fusion.29
  24.6 57.3 %all-gather.3.cloned.1.call-done = f32[96,320,32]{1,2,0:T(8,128)} async-done(((f32[3,320,32]{1,2,0:T(8,128)}), f32[96,320,32]{1,2,0:T(8,128)}) %all-gather.3.cloned.1.call-update) | async-done | bytes 3932176 | tf_op jit(solution)/shard_map/all_gather | solution.py:26
  81.8 2.8 reduce_sum.36
  84.7 0.3 fusion.32
  85.0 0.1 copy.15
  85.1 8.8 %custom-call.7 = f32[3,32,32]{2,1,0:T(8,128)S(1)} custom-call(f32[3,32,32]{2,1,0:T(8,128)S(1)} %fusion.26), custom_call_target="Cholesky" | custom-call | tf_op jit(solution)/shard_map/jit(cholesky)/cholesky | solution.py:28
  93.9 0.1 compare_reduce_fusion
  94.0 0.1 select_bitcast_fusion
  94.1 7.4 %custom-call.8 = f32[3,1,32,32]{2,3,1,0:T(8,128)S(1)} custom-call(f32[3,1,32,32]{3,2,1,0:T(8,128)S(1)} %select_bitcast_fusion), custom_call_target="InvertDiagBlocksLowerTriangular" | custom-call | tf_op jit(solution)/shard_map/triangular_solve | solution.py:29
  101.5 0.3 fusion.24
  101.8 0.0 copy-done.2
  101.8 4.8 %fusion = f32[3,960,32]{1,2,0:T(8,128)S(1)} fusion(f32[3,320,32]{1,2,0:T(8,128)S(1)} %fusion.24, f32[1,3,320,960]{3,2,1,0:T(8,128)} %param.8, bf16[1,3,320,960]{3,2,1,0:T(8,128)(2,1)S(1)} %copy-done.2), kind=kOutput, calls=%fused_computation.1 | convolution fusion | flops 355737600 | bytes 6021120 | tf_op jit(solution)/shard_map/mkd,mkr->mdr/dot_general | solution.py:32
  106.6 0.0 copy-start.4
  106.6 0.0 copy-start.6
  106.7 0.0 copy-start.7
  106.7 0.0 copy-start.8
  106.7 6.3 %fusion.5 = bf16[1,3,320,960]{3,2,1,0:T(8,128)(2,1)} fusion(f32[3,320,32]{1,2,0:T(8,128)S(1)} %fusion.24, f32[3,960,32]{1,2,0:T(8,128)S(1)} %fusion, f32[1,3,320,960]{3,2,1,0:T(8,128)} %param.8, bf16[1,3,320,960]{3,2,1,0:T(8,128)(2,1)S(1)} %copy-done.2), kind=kOutput, calls=%fused_computation.9 | convolution fusion | flops 357580800 | bytes 7864320 | tf_op jit(solution)/shard_map/mkr,mdr->mkd/dot_general | solution.py:34
  113.0 0.0 copy-done.4
  113.0 0.0 all-reduce.4.cloned.1.call-start
  113.0 0.7 all-reduce.4.cloned.1.call-update
  113.8 0.2 all-reduce.6.cloned.1.call-start
  114.0 0.0 copy-done.6
  114.0 0.0 copy-done.7
  114.0 0.0 copy-done.8
  114.0 0.2 select_reduce_fusion.2
  114.2 0.7 fusion.30
  118.6 0.0 copy-start.3
  118.6 127.4 %all-reduce.4.cloned.1.call-done = f32[3,960,32]{1,2,0:T(8,128)} async-done(((f32[3,960,32]{1,2,0:T(8,128)}), f32[3,960,32]{1,2,0:T(8,128)}) %all-reduce.4.cloned.1.call-update) | async-done | bytes 368656 | tf_op jit(solution)/shard_map/psum | solution.py:33
  246.0 4.3 %fusion.33 = f32[3,320,960]{2,1,0:T(8,128)S(1)} fusion(f32[3,320,32]{1,2,0:T(8,128)S(1)} %fusion.24, f32[3,960,32]{1,2,0:T(8,128)} %all-reduce.4.cloned.1.call-done), kind=kOutput, calls=%fused_computation.60 | convolution fusion | flops 353894400 | bytes 4177920 | tf_op jit(solution)/shard_map/mkr,mdr->mkd/dot_general | solution.py:36
  250.3 0.0 copy-start.1
  250.3 3.9 fusion.19
  254.2 0.0 copy-done.1
  254.2 0.0 all-reduce.6.cloned.1.call-update
  254.2 0.6 compare_and_fusion.2
  254.9 1.3 compare_and_fusion
  256.2 4.8 %add_bitcast_fusion.2 = (f32[320,960]{1,0:T(8,128)S(1)}, f32[320,960]{1,0:T(8,128)S(1)}, f32[320,960]{1,0:T(8,128)S(1)}) fusion(f32[3,320,960]{2,1,0:T(8,128)} %copy-done.1, f32[]{:T(128)} %bitcast.9, bf16[2,320,960]{2,1,0:T(8,128)(2,1)S(1)} %copy-done.3, s32[]{:T(128)S(6)} %select_n.55, s32[]{:T(128)S(6)} %select_n.58, f32[]{:T(128)} %bitcast.16, ...), kind=kLoop, calls=%fused_computation.27 | loop fusion | flops 2764800 | bytes 9216024 | tf_op jit(solution)/shard_map/jit(_where)/broadcast_in_dim | solution.py:51
  261.0 1.7 add_convert_fusion
  262.7 124.9 %all-reduce.6.cloned.1.call-done = (bf16[1,320,960]{2,1,0:T(8,128)(2,1)}, bf16[1,320,960]{2,1,0:T(8,128)(2,1)}, bf16[1,320,960]{2,1,0:T(8,128)(2,1)}) async-done(((bf16[1,320,960]{2,1,0:T(8,128)(2,1)}, bf16[1,320,960]{2,1,0:T(8,128)(2,1)}, bf16[1,320,960]{2,1,0:T(8,128)(2,1)}), (bf16[1,320,960]{2,1,0:T(8,128)(2,1)}, bf16[1,320,960]{2,1,0:T(8,128)(2,1)}, ...) | async-done | bytes 1843216 | tf_op jit(solution)/shard_map/psum | solution.py:9
  387.6 3.0 maximum_bitcast_fusion
  (6 shorter events, 0.1 us)
Async XLA Ops:
  7.2 1.0 copy-start
  7.2 8.2 %copy-start.5 = (s32[3]{0:T(128)S(1)}, s32[3]{0:T(128)}, u32[]{:S(2)}) copy-start(s32[3]{0:T(128)} %param.11) | copy-start | bytes 40
  7.2 74.7 %all-gather.3.cloned.1.call-start = ((), (), s32[]{:S(2)}) async-start(), calls=%async_computation.1 | async-start | bytes 4866048 | tf_op jit(solution)/shard_map/all_gather | solution.py:26
  81.8 20.0 %copy-start.2 = (bf16[1,3,320,960]{3,2,1,0:T(8,128)(2,1)S(1)}, bf16[1,3,320,960]{3,2,1,0:T(8,128)(2,1)}, u32[]{:S(2)}) copy-start(bf16[1,3,320,960]{3,2,1,0:T(8,128)(2,1)} %param.9) | copy-start | bytes 5529604
  106.6 6.4 %copy-start.4 = (f32[3,960,32]{1,2,0:T(8,128)}, f32[3,960,32]{1,2,0:T(8,128)S(1)}, u32[]{:S(2)}) copy-start(f32[3,960,32]{1,2,0:T(8,128)S(1)} %fusion) | copy-start | bytes 1105924
  106.6 7.3 %copy-start.6 = (f32[4]{0:T(128)S(1)}, f32[4]{0:T(128)}, u32[]{:S(2)}) copy-start(f32[4]{0:T(128)} %param.13) | copy-start | bytes 52
  106.7 7.3 %copy-start.7 = (s32[3]{0:T(128)S(1)}, s32[3]{0:T(128)}, u32[]{:S(2)}) copy-start(s32[3]{0:T(128)} %param.12) | copy-start | bytes 40
  106.7 7.3 %copy-start.8 = (f32[4]{0:T(128)S(1)}, f32[4]{0:T(128)}, u32[]{:S(2)}) copy-start(f32[4]{0:T(128)} %param.14) | copy-start | bytes 52
  113.0 133.0 %all-reduce.4.cloned.1.call-start = ((), (), s32[]{:S(2)}) async-start(), calls=%async_computation | async-start | bytes 786432 | tf_op jit(solution)/shard_map/psum | solution.py:33
  113.8 273.9 %all-reduce.6.cloned.1.call-start = ((), (), s32[]{:S(2)}) async-start(), calls=%async_computation.2 | async-start | bytes 3932160 | tf_op jit(solution)/shard_map/psum | solution.py:9
  118.6 131.7 %copy-start.3 = (bf16[2,320,960]{2,1,0:T(8,128)(2,1)S(1)}, bf16[2,320,960]{2,1,0:T(8,128)(2,1)}, u32[]{:S(2)}) copy-start(bf16[2,320,960]{2,1,0:T(8,128)(2,1)} %param.15) | copy-start | bytes 3686404
  250.3 3.9 copy-start.1
Sparse Core Ops, SparseCore 0:
  15.5 66.3 all-gather.2
  119.7 126.2 all-reduce.3
  254.4 133.2 all-reduce.5
